TPU v7x, 128 devices: a whole 4x4x4 slice. The times are simulated.
128 devices in a mesh: pb: 4 (over z_hi, core), ka: 32 (over z_lo, y, x).
Axes of the slice: x: 4, y: 4, z: 4 (z_hi: 2, z_lo: 2; z = z_hi * 2 + z_lo), core: 2. Of those that a mesh axis runs over, the one named last changes fastest.
Arguments:
- vertex_ladder: float32 [2, 16, 1024, 1024], P(None, 'pb', 'ka'), may hold values from -6 to 6
- vertex_cross_a: float32 [2, 16, 1024, 1024], P(None, 'pb', 'ka'), may hold values from -6 to 6
- vertex_cross_b: float32 [2, 16, 1024, 1024], P(None, 'pb', 'ka'), may hold values from -6 to 6
- bubble: float32 [2, 16, 1024], P(None, 'pb'), may hold values from -0.072 to 0.072
- row_maps: int32 [2, 16, 1024], replicated, may hold values from 0 to 16383, as said below
- col_maps: int32 [2, 1024], replicated, may hold values from 0 to 1023, each once within a row
Outputs:
- ladder_out: float32 [2, 16, 1024, 1024], P(None, 'pb', 'ka')
- crossed_a: float32 [2, 16, 1024, 1024], P(None, 'pb', 'ka')
- crossed_b: float32 [2, 16, 1024, 1024], P(None, 'pb', 'ka')
Inputs may be any that keep to these rules, and one draw needn't show every extreme that they name: `row_maps`: each of the two maps is a permutation of all 16384 rows. A device holds the rows of its bosonic indices (index of pb) and its first fermionic indices (index of ka); the 128 rows of one device take exactly 1 of their source rows from each device.
All inputs are finite; a program needn't handle non-finite values.
Results may differ from a plain program's by a relative error of at most 0.007.
Values may be sent and summed in bfloat16 or wider, within the bound.
A program may use at most 64 MiB of HBM per device.

v0:
```python
import jax
import jax.numpy as jnp
from jax import lax
from jax.sharding import PartitionSpec as P

LADDER = 6


def in_one_piece(arrays, axis, split_dim, concat_dim, along):
    ends, at = ([], 0)
    for a in arrays[:-1]:
        at += a.shape[along]
        ends.append(at)
    both = jnp.concatenate(arrays, axis=along)
    return tuple(
        jnp.split(
            lax.all_to_all(both, axis, split_axis=split_dim, concat_axis=concat_dim, tiled=True),
            ends,
            axis=along,
        )
    )


def ladder_rows(vertex_rows, bubble_q, gathered):
    col_count = gathered.shape[2]
    row_count = vertex_rows.shape[1]
    right_op = jnp.concatenate([gathered[0], gathered[1]], 1)
    current = vertex_rows
    for _ in range(LADDER):
        scaled_re = current[0] * bubble_q[0][None, :] - current[1] * bubble_q[1][None, :]
        scaled_im = current[0] * bubble_q[1][None, :] + current[1] * bubble_q[0][None, :]
        left_op = jnp.concatenate([scaled_re, scaled_im], 0).astype(jnp.bfloat16)
        product = jnp.dot(left_op, right_op, preferred_element_type=jnp.float32)
        real_part = product[:row_count, :col_count] - product[row_count:, col_count:]
        imag_part = product[:row_count, col_count:] + product[row_count:, :col_count]
        current = vertex_rows + jnp.stack([real_part, imag_part])
    return current


def per_device(vertex_ladder, vertex_cross_a, vertex_cross_b, bubble, row_maps, col_maps):
    q_local = vertex_ladder.shape[1]
    row_count = vertex_ladder.shape[2]
    col_count = vertex_ladder.shape[3]
    gamma_low = vertex_ladder.astype(jnp.bfloat16)
    whole_low = lax.all_gather(gamma_low, "ka", axis=2, tiled=True)

    def per_whole(loop_state, scan_items):
        vertex_rows, gathered, bubble_q = scan_items
        return (loop_state, ladder_rows(vertex_rows, bubble_q, gathered))

    _, stacked = lax.scan(
        per_whole,
        jnp.int32(0),
        (
            jnp.moveaxis(vertex_ladder, 1, 0),
            jnp.moveaxis(whole_low, 1, 0),
            jnp.moveaxis(bubble, 1, 0),
        ),
    )
    ladder_out = jnp.moveaxis(stacked, 0, 1)
    local_count = q_local * row_count
    reducible = (ladder_out - vertex_ladder).reshape(2, local_count, col_count)
    pb_count = lax.axis_size("pb")
    ka_count = lax.axis_size("ka")
    dev_count = pb_count * ka_count
    per_peer = local_count // dev_count
    my_device = lax.axis_index("pb") * ka_count + lax.axis_index("ka")
    my_bos = lax.axis_index("pb") * q_local + jnp.arange(q_local, dtype=jnp.int32)
    my_fer = lax.axis_index("ka") * row_count + jnp.arange(row_count, dtype=jnp.int32)
    my_rows = (my_bos[:, None] * col_count + my_fer[None, :]).reshape(-1)
    slot_ids = jnp.arange(per_peer, dtype=jnp.int32)

    def device_of(global_rows):
        return global_rows // col_count // q_local * ka_count + global_rows % col_count // row_count

    def prepare(table_flat):
        by_device = (
            table_flat.reshape(pb_count, q_local, ka_count, row_count)
            .transpose(0, 2, 1, 3)
            .reshape(dev_count, local_count)
        )
        mine = (device_of(by_device) == my_device).astype(jnp.int32)
        rank = jnp.cumsum(mine, 1) - 1
        source_local = (
            by_device // col_count % q_local * row_count + by_device % col_count % row_count
        )
        hits = mine[:, :, None] * (rank[:, :, None] == slot_ids[None, None, :]).astype(jnp.int32)
        send_index = jnp.sum(hits * source_local[:, :, None], 1).reshape(-1)
        return jnp.take(reducible, send_index, axis=1)

    def place(table_flat, received, column_map):
        source = table_flat[my_rows]
        source_dev = device_of(source)
        onehot = (source_dev[:, None] == jnp.arange(dev_count, dtype=jnp.int32)[None, :]).astype(
            jnp.int32
        )
        slot_index = jnp.sum((jnp.cumsum(onehot, 0) - onehot) * onehot, 1)
        picked = jnp.take(received, source_dev * per_peer + slot_index, axis=1)
        selector = (jnp.arange(col_count, dtype=jnp.int32)[:, None] == column_map[None, :]).astype(
            jnp.float32
        )
        picked = jnp.einsum("prk,km->prm", picked, selector, precision=lax.Precision.HIGHEST)
        return picked.reshape(2, q_local, row_count, col_count)

    table_a = row_maps[0].reshape(-1)
    table_b = row_maps[1].reshape(-1)
    send_a = prepare(table_a)
    send_b = prepare(table_b)
    recv_a, recv_b = in_one_piece((send_a, send_b), ("pb", "ka"), 1, 1, 0)
    crossed_a = vertex_cross_a + place(table_a, recv_a, col_maps[0])
    crossed_b = vertex_cross_b + place(table_b, recv_b, col_maps[1])
    return (ladder_out, crossed_a, crossed_b)


def solution(mesh):
    return jax.shard_map(
        per_device,
        mesh=mesh,
        in_specs=(
            P(None, "pb", "ka", None),
            P(None, "pb", "ka", None),
            P(None, "pb", "ka", None),
            P(None, "pb", None),
            P(),
            P(),
        ),
        out_specs=(P(None, "pb", "ka", None), P(None, "pb", "ka", None), P(None, "pb", "ka", None)),
        check_vma=False,
    )
```

profile of v0, /device:TPU:0, one launch (start us, length us, event | category | flops | bytes accessed | tf_op | source)
XLA Modules:
  0.0 306.2 jit_solution(12772516117283020420)
XLA Ops:
  7.2 2.1 copy.49
  9.4 1.3 copy.50
  10.9 0.2 copy.51
  11.1 0.2 reshape.234
  11.5 0.2 reduce_window_sum.35
  12.0 0.2 copy.52
  12.2 0.2 reshape.233
  12.4 0.1 fusion.93
  12.6 0.2 reduce_window_sum.34
  13.1 4.7 %fusion.64 = (s32[4,32]{1,0:T(4,128)S(1)}, s32[4,32]{1,0:T(4,128)S(1)}) fusion(pred[4,32,4,32]{3,2,1,0:T(4,128)(4,1)S(1)} %eq.118, s32[]{:T(128)S(6)} %add.312, s32[4,4,32,32]{3,2,1,0:T(8,128)S(1)} %reshape_reshape_squeeze.7, pred[4,32,4,32]{3,2,1,0:T(4,128)(4,1)S(1)} %eq.113, s32[4,4,32,32]{3,2,1,0:T(8,128)S(1)} %reshape_reshape_squeeze.6), kind=kLoop, calls=%fused_computation.162 | loop fusion | flops 2162432 | bytes 164868 | tf_op jit(solution)/shard_map/reduce_sum | solution.py:88
  18.2 187.6 %all-gather.2.cloned.1.call-done = bf16[2,4,1024,1024]{3,2,0,1:T(8,128)(2,1)} async-done(((bf16[2,4,32,1024]{3,2,0,1:T(8,128)(2,1)}), bf16[2,4,1024,1024]{3,2,0,1:T(8,128)(2,1)}) %all-gather.2.cloned.1.call-update) | async-done | bytes 16777232 | tf_op jit(solution)/shard_map/all_gather | solution.py:45
  205.9 34.4 %while.10 = (s32[]{:T(128)}, f32[4,2,32,1024]{3,2,0,1:T(8,128)S(1)}, f32[4,2,32,1024]{3,2,1,0:T(8,128)S(1)}, f32[4,2,1024]{2,1,0:T(2,128)S(1)}, bf16[4,2,1024,10...) while((s32[]{:T(128)}, f32[4,2,32,1024]{3,2,0,1:T(8,128)S(1)}, f32[4,2,32,1024]{3,2,1,0:T(8,128)S(1)}, ...), condition=%wide.region_1.2_spmd, body=%wide.region_0.1_spmd.sunk | while | flops 1665269760 | bytes 49348760 | solution.py:51
  205.9 2.7 dynamic-slice_bitcast_fusion.5
  208.7 0.8 fusion.124
  209.6 0.8 fusion.126
  210.6 0.8 fusion.128
  211.6 0.8 fusion.130
  212.6 0.8 fusion.132
  213.6 0.8 fusion.134
  214.6 2.7 dynamic-slice_bitcast_fusion.5
  217.3 0.8 fusion.124
  218.2 0.8 fusion.126
  219.2 0.8 fusion.128
  220.2 0.8 fusion.130
  221.2 0.8 fusion.132
  222.2 0.8 fusion.134
  223.2 2.7 dynamic-slice_bitcast_fusion.5
  225.9 0.8 fusion.124
  226.8 0.8 fusion.126
  227.8 0.8 fusion.128
  228.8 0.8 fusion.130
  229.8 0.8 fusion.132
  230.8 0.8 fusion.134
  231.8 2.7 dynamic-slice_bitcast_fusion.5
  234.5 0.8 fusion.124
  235.4 0.8 fusion.126
  236.4 0.8 fusion.128
  237.4 0.8 fusion.130
  238.4 0.8 fusion.132
  239.3 0.8 fusion.134
  240.3 0.2 bitcast_subtract_fusion
  240.5 0.8 copy.26
  241.3 1.7 gather_fusion.3
  243.0 1.7 gather_fusion.2
  244.7 0.5 select_bitcast_fusion.2
  245.2 0.5 select_bitcast_fusion.3
  245.8 2.3 pad_maximum_fusion.7
  248.0 7.3 %all-to-all-start = ((f32[4,128,1024]{2,0,1:T(4,128)}), f32[4,128,1024]{2,0,1:T(4,128)S(1)}, u32[]{:S(2)}, u32[]{:S(2)}) async-start(f32[4,128,1024]{2,0,1:T(4,128)} %pad_maximum_fusion.7), calls=%async_computation | async-start | bytes 4194304 | tf_op jit(solution)/shard_map/all_to_all | solution.py:17
  255.4 1.1 gather_fusion
  256.6 0.2 reduce_window_sum.36
  256.8 1.1 gather_fusion.1
  258.1 0.2 reduce_window_sum.37
  258.3 0.2 select_reduce_fusion.1
  258.5 0.2 select_reduce_fusion
  258.7 26.1 %all-to-all-done = f32[4,128,1024]{2,0,1:T(4,128)S(1)} async-done(((f32[4,128,1024]{2,0,1:T(4,128)}), f32[4,128,1024]{2,0,1:T(4,128)S(1)}, u32[]{:S(2)}, u32[]{:S(2)}) %all-to-all-start) | async-done | bytes 2097184 | tf_op jit(solution)/shard_map/all_to_all | solution.py:17
  284.8 1.8 fusion.97
  286.6 3.0 gather_fusion.4
  289.6 0.5 select_bitcast_fusion.1
  290.2 2.3 fusion.45
  292.5 1.1 add.337
  293.6 1.7 gather_fusion.5
  295.3 0.5 select_bitcast_fusion
  295.8 2.3 fusion.48
  298.2 1.1 add.341
  (131 shorter events, 4.6 us)
Async XLA Ops:
  7.2 3.5 %copy-start.5 = (f32[2,4,1024]{2,1,0:T(4,128)S(1)}, f32[2,4,1024]{2,1,0:T(4,128)}, u32[]{:S(2)}) copy-start(f32[2,4,1024]{2,1,0:T(4,128)} %param.13) | copy-start | bytes 98308
  7.2 3.6 %copy-start.4 = (s32[2,16,1024]{2,1,0:T(8,128)S(1)}, s32[2,16,1024]{2,1,0:T(8,128)}, u32[]{:S(2)}) copy-start(s32[2,16,1024]{2,1,0:T(8,128)} %param.14) | copy-start | bytes 393220
  7.2 198.7 %all-gather.2.cloned.1.call-start = ((), (), s32[]{:S(2)}) async-start(), calls=%async_computation.1 | async-start | bytes 17301504 | tf_op jit(solution)/shard_map/all_gather | solution.py:45
  205.8 34.5 %copy-start = (f32[2,4,32,1024]{3,2,1,0:T(8,128)S(1)}, f32[2,4,32,1024]{3,2,1,0:T(8,128)}, u32[]{:S(2)}) copy-start(f32[2,4,32,1024]{3,2,1,0:T(8,128)} %param.10) | copy-start | bytes 3145732
  240.3 1.0 copy-start.3
  245.7 13.0 %copy-start.6 = (s32[2,1024]{1,0:T(2,128)S(1)}, s32[2,1024]{1,0:T(2,128)}, u32[]{:S(2)}) copy-start(s32[2,1024]{1,0:T(2,128)} %param.15) | copy-start | bytes 24580
  248.0 36.8 %all-to-all-start = ((f32[4,128,1024]{2,0,1:T(4,128)}), f32[4,128,1024]{2,0,1:T(4,128)S(1)}, u32[]{:S(2)}, u32[]{:S(2)}) async-start(f32[4,128,1024]{2,0,1:T(4,128)} %pad_maximum_fusion.7), calls=%async_computation | async-start | bytes 4194304 | tf_op jit(solution)/shard_map/all_to_all | solution.py:17
  286.6 5.9 %copy-start.1 = (f32[2,4,32,1024]{3,2,1,0:T(8,128)S(1)}, f32[2,4,32,1024]{3,2,1,0:T(8,128)}, u32[]{:S(2)}) copy-start(f32[2,4,32,1024]{3,2,1,0:T(8,128)} %param.11) | copy-start | bytes 3145732
  293.6 4.6 %copy-start.2 = (f32[2,4,32,1024]{3,2,1,0:T(8,128)S(1)}, f32[2,4,32,1024]{3,2,1,0:T(8,128)}, u32[]{:S(2)}) copy-start(f32[2,4,32,1024]{3,2,1,0:T(8,128)} %param.12) | copy-start | bytes 3145732
Sparse Core Ops, SparseCore 0:
  10.2 195.5 all-gather.1
where the time goes:
time: 306 us
  waiting for transfers between devices  214 us (70%)
  local copies, waits for them, and re-layouts  29.1 us (10%)
  matrix products  24.9 us (8%)
  other arithmetic  16 us (5%)
  between operations  14.5 us (5%)
  starting transfers between devices  7.32 us (2%)
    all_gather x1, waiting for transfers between devices, per_device(): whole_low = lax.all_gather(gamma_low, 'ka', axis=2, tiled=True)  188 us
    all_to_all x1, waiting for transfers between devices, in_one_piece(): lax.all_to_all(both, axis, split_axis=split_dim, concat_axis=concat_dim,...  26.1 us
    dot_general x24, matrix products, ladder_rows(): product = jnp.dot(left_op, right_op, preferred_element_type=jnp.float32)  20.3 us
    squeeze x4, local copies, waits for them, and re-layouts, ladder_rows(): right_op = jnp.concatenate([gathered[0], gathered[1]], 1)  10.8 us
    all_to_all x1, starting transfers between devices, in_one_piece(): lax.all_to_all(both, axis, split_axis=split_dim, concat_axis=concat_dim,...  7.28 us
  transfers between devices with their start and end apart: 2, of which 2 were waited for; matrix products, arithmetic and copies ran while one was open for 4% of the time, Pallas kernels for 0%

commit v1 on v0

--- a/solution.py
+++ b/solution.py
@@ -42,7 +42,9 @@
     row_count = vertex_ladder.shape[2]
     col_count = vertex_ladder.shape[3]
     gamma_low = vertex_ladder.astype(jnp.bfloat16)
-    whole_low = lax.all_gather(gamma_low, "ka", axis=2, tiled=True)
+    whole_low = jnp.concatenate(
+        lax.all_to_all(jnp.stack([gamma_low] * lax.axis_size("ka")), "ka", 0, 0), axis=2
+    )
 
     def per_whole(loop_state, scan_items):
         vertex_rows, gathered, bubble_q = scan_items

time: 306 us -> 422 us (1.38)
  waiting for transfers between devices: 214 us -> 288 us
  starting transfers between devices: 7.32 us -> 41.7 us
  local copies, waits for them, and re-layouts: 29.1 us -> 47.5 us
  between operations: 14.5 us -> 1.12 us
    all_to_all x0 -> x1, waiting for transfers between devices: none -> 262 us  [per_device(): lax.all_to_all(jnp.stack([gamma_low] * lax.axis_size('ka')), 'ka', 0, 0)]
    all_gather x1 -> x0, waiting for transfers between devices: 188 us -> none  [per_device(): whole_low = lax.all_gather(gamma_low, 'ka', axis=2, tiled=True)]
    all_to_all x1, starting transfers between devices: 7.28 us -> 32.7 us  [in_one_piece(): lax.all_to_all(both, axis, split_axis=split_dim, concat_axis=concat_dim,...]
    all_to_all x0 -> x1, local copies, waits for them, and re-layouts: none -> 14.2 us  [per_device(): lax.all_to_all(jnp.stack([gamma_low] * lax.axis_size('ka')), 'ka', 0, 0)]
    dynamic_slice x0 -> x4, local copies, waits for them, and re-layouts: none -> 10.6 us  [per_device(): lax.scan(per_whole, jnp.int32(0), (jnp.moveaxis(vertex_ladder, 1, 0), jnp...]
    all_to_all x0 -> x1, starting transfers between devices: none -> 9.02 us  [per_device(): lax.all_to_all(jnp.stack([gamma_low] * lax.axis_size('ka')), 'ka', 0, 0)]
    squeeze x4, local copies, waits for them, and re-layouts: 10.8 us -> 1.77 us  [ladder_rows(): right_op = jnp.concatenate([gathered[0], gathered[1]], 1)]
    another operation x0 -> x1, local copies, waits for them, and re-layouts: none -> 5.97 us  [per_device(): jnp.stack([gamma_low] * lax.axis_size('ka'))]
  transfers between devices with their start and end apart: 2 -> 2, of which waited for: 2 -> 2; matrix products, arithmetic and copies ran while one was open for 4% -> 3% of each run, Pallas kernels for 0% -> 0%
where the time goes in v1:
time: 422 us; the launch traced here: 421 us
  waiting for transfers between devices  288 us (68%)
  local copies, waits for them, and re-layouts  47.5 us (11%)
  starting transfers between devices  41.7 us (10%)
  matrix products  24.8 us (6%)
  other arithmetic  17.2 us (4%)
    all_to_all x1, waiting for transfers between devices, per_device(): lax.all_to_all(jnp.stack([gamma_low] * lax.axis_size('ka')), 'ka', 0, 0)  262 us
    all_to_all x1, starting transfers between devices, in_one_piece(): lax.all_to_all(both, axis, split_axis=split_dim, concat_axis=concat_dim,...  32.7 us
    all_to_all x1, waiting for transfers between devices, in_one_piece(): lax.all_to_all(both, axis, split_axis=split_dim, concat_axis=concat_dim,...  26.3 us
    dot_general x24, matrix products, ladder_rows(): product = jnp.dot(left_op, right_op, preferred_element_type=jnp.float32)  20.2 us
    all_to_all x1, local copies, waits for them, and re-layouts, per_device(): lax.all_to_all(jnp.stack([gamma_low] * lax.axis_size('ka')), 'ka', 0, 0)  14.2 us
    dynamic_slice x4, local copies, waits for them, and re-layouts, per_device(): lax.scan(per_whole, jnp.int32(0), (jnp.moveaxis(vertex_ladder, 1, 0), jnp...  10.6 us
    all_to_all x1, starting transfers between devices, per_device(): lax.all_to_all(jnp.stack([gamma_low] * lax.axis_size('ka')), 'ka', 0, 0)  9.02 us
  transfers between devices with their start and end apart: 2, of which 2 were waited for; matrix products, arithmetic and copies ran while one was open for 3% of the time, Pallas kernels for 0%

profile of v1, /device:TPU:0, one launch (start us, length us, event | category | flops | bytes accessed | tf_op | source)
XLA Modules:
  0.0 421.4 jit_solution(66641973159477867)
XLA Ops:
  0.6 1.3 convert_element_type.35
  2.0 6.0 %stack.38 = bf16[32,2,4,32,1024]{4,3,1,2,0:T(8,128)(2,1)} broadcast(bf16[2,4,32,1024]{3,2,0,1:T(8,128)(2,1)S(1)} %copy.47), dimensions={1,2,3,4} | broadcast | bytes 17301504 | tf_op jit(solution)/shard_map/stack | solution.py:46
  8.0 9.0 %all-to-all-start = ((bf16[32,2,4,32,1024]{4,3,1,2,0:T(8,128)(2,1)}), bf16[32,2,4,32,1024]{4,3,1,2,0:T(8,128)(2,1)}, u32[]{:S(2)}, u32[]{:S(2)}) async-start(bf16[32,2,4,32,1024]{4,3,1,2,0:T(8,128)(2,1)} %stack.38), calls=%async_computation | async-start | bytes 33554432 | tf_op jit(solution)/shard_map/all_to_all | solution.py:46
  17.3 0.2 copy.79
  17.9 0.2 reduce_window_sum.34
  18.4 0.2 copy.78
  19.0 0.2 reduce_window_sum.35
  19.5 4.7 %fusion.64 = (s32[4,32]{1,0:T(4,128)S(1)}, s32[4,32]{1,0:T(4,128)S(1)}) fusion(pred[4,32,4,32]{3,2,1,0:T(4,128)(4,1)S(1)} %eq.118, s32[]{:T(128)S(6)} %add.312, s32[4,4,32,32]{3,2,1,0:T(8,128)S(1)} %reshape_reshape_squeeze.7, pred[4,32,4,32]{3,2,1,0:T(4,128)(4,1)S(1)} %eq.113, s32[4,4,32,32]{3,2,1,0:T(8,128)S(1)} %reshape_reshape_squeeze.6), kind=kLoop, calls=%fused_computation.162 | loop fusion | flops 2162432 | bytes 164868 | tf_op jit(solution)/shard_map/reduce_sum | solution.py:90
  24.6 261.8 %all-to-all-done = bf16[32,2,4,32,1024]{4,3,1,2,0:T(8,128)(2,1)} async-done(((bf16[32,2,4,32,1024]{4,3,1,2,0:T(8,128)(2,1)}), bf16[32,2,4,32,1024]{4,3,1,2,0:T(8,128)(2,1)}, u32[]{:S(2)}, u32[]{:S(2)}) %all-to-all-start) | async-done | bytes 16777248 | tf_op jit(solution)/shard_map/all_to_all | solution.py:46
  286.5 14.2 %copy.48 = bf16[32,2,4,32,1024]{4,3,0,2,1:T(8,128)(2,1)} copy(bf16[32,2,4,32,1024]{4,3,1,2,0:T(8,128)(2,1)} %all-to-all-done) | data formatting | bytes 33554432 | tf_op jit(solution)/shard_map/all_to_all | solution.py:46
  300.6 36.1 %while.10 = (s32[]{:T(128)}, f32[4,2,32,1024]{3,2,0,1:T(8,128)S(1)}, f32[4,2,32,1024]{3,2,1,0:T(8,128)S(1)}, f32[4,2,1024]{2,1,0:T(2,128)S(1)}, bf16[4,2,1024,10...) while((s32[]{:T(128)}, f32[4,2,32,1024]{3,2,0,1:T(8,128)S(1)}, f32[4,2,32,1024]{3,2,1,0:T(8,128)S(1)}, ...), condition=%wide.region_1.2_spmd, body=%wide.region_0.1_spmd.sunk | while | flops 1665269760 | bytes 57737356 | solution.py:53
  300.7 2.6 dynamic-slice_bitcast_fusion.4
  303.3 0.4 slice_bitcast_fusion.15
  303.8 0.8 fusion.124
  304.8 0.8 fusion.126
  305.7 0.8 fusion.128
  306.7 0.8 fusion.130
  307.7 0.8 fusion.132
  308.7 0.8 fusion.134
  309.7 2.6 dynamic-slice_bitcast_fusion.4
  312.3 0.4 slice_bitcast_fusion.15
  312.8 0.8 fusion.124
  313.8 0.8 fusion.126
  314.7 0.8 fusion.128
  315.7 0.8 fusion.130
  316.7 0.8 fusion.132
  317.6 0.8 fusion.134
  318.7 2.6 dynamic-slice_bitcast_fusion.4
  321.3 0.4 slice_bitcast_fusion.15
  321.8 0.8 fusion.124
  322.7 0.8 fusion.126
  323.7 0.8 fusion.128
  324.7 0.8 fusion.130
  325.7 0.8 fusion.132
  326.6 0.8 fusion.134
  327.7 2.6 dynamic-slice_bitcast_fusion.4
  330.3 0.4 slice_bitcast_fusion.15
  330.7 0.8 fusion.124
  331.7 0.8 fusion.126
  332.7 0.8 fusion.128
  333.7 0.8 fusion.130
  334.6 0.8 fusion.132
  335.6 0.8 fusion.134
  336.9 0.8 copy.54
  337.7 1.7 gather_fusion.2
  339.4 1.7 gather_fusion.3
  341.1 0.5 select_bitcast_fusion.3
  341.6 0.5 select_bitcast_fusion.2
  342.2 2.3 pad_maximum_fusion.7
  344.5 32.7 %all-to-all-start.1 = ((f32[4,128,1024]{2,0,1:T(4,128)}), f32[4,128,1024]{2,0,1:T(4,128)S(1)}, u32[]{:S(2)}, u32[]{:S(2)}) async-start(f32[4,128,1024]{2,0,1:T(4,128)} %pad_maximum_fusion.7), calls=%async_computation.1 | async-start | bytes 4194304 | tf_op jit(solution)/shard_map/all_to_all | solution.py:17
  377.2 1.1 gather_fusion.1
  378.5 0.2 reduce_window_sum.37
  378.7 1.1 gather_fusion
  380.0 0.2 reduce_window_sum.36
  380.6 26.3 %all-to-all-done.1 = f32[4,128,1024]{2,0,1:T(4,128)S(1)} async-done(((f32[4,128,1024]{2,0,1:T(4,128)}), f32[4,128,1024]{2,0,1:T(4,128)S(1)}, u32[]{:S(2)}, u32[]{:S(2)}) %all-to-all-start.1) | async-done | bytes 2097184 | tf_op jit(solution)/shard_map/all_to_all | solution.py:17
  406.9 1.8 fusion.97
  408.7 3.0 gather_fusion.5
  411.7 0.5 select_bitcast_fusion
  412.2 2.3 fusion.48
  414.6 1.1 add.341
  415.7 1.7 gather_fusion.4
  417.4 0.5 select_bitcast_fusion.1
  417.9 2.3 fusion.45
  420.3 1.1 add.337
  (139 shorter events, 5.6 us)
Async XLA Ops:
  8.0 9.0 %copy-start = (f32[2,4,32,1024]{3,2,1,0:T(8,128)S(1)}, f32[2,4,32,1024]{3,2,1,0:T(8,128)}, u32[]{:S(2)}) copy-start(f32[2,4,32,1024]{3,2,1,0:T(8,128)} %param.10) | copy-start | bytes 3145732
  8.0 9.2 %copy-start.5 = (s32[2,16,1024]{2,1,0:T(8,128)S(1)}, s32[2,16,1024]{2,1,0:T(8,128)}, u32[]{:S(2)}) copy-start(s32[2,16,1024]{2,1,0:T(8,128)} %param.14) | copy-start | bytes 393220
  8.0 278.5 %all-to-all-start = ((bf16[32,2,4,32,1024]{4,3,1,2,0:T(8,128)(2,1)}), bf16[32,2,4,32,1024]{4,3,1,2,0:T(8,128)(2,1)}, u32[]{:S(2)}, u32[]{:S(2)}) async-start(bf16[32,2,4,32,1024]{4,3,1,2,0:T(8,128)(2,1)} %stack.38), calls=%async_computation | async-start | bytes 33554432 | tf_op jit(solution)/shard_map/all_to_all | solution.py:46
  17.0 7.3 %copy-start.6 = (f32[2,4,1024]{2,1,0:T(4,128)S(1)}, f32[2,4,1024]{2,1,0:T(4,128)}, u32[]{:S(2)}) copy-start(f32[2,4,1024]{2,1,0:T(4,128)} %param.13) | copy-start | bytes 98308
  24.6 276.0 %copy-start.3 = (f32[4,2,32,1024]{3,2,0,1:T(8,128)S(1)}, f32[4,2,32,1024]{3,2,0,1:T(8,128)}, u32[]{:S(2)}) copy-start(f32[4,2,32,1024]{3,2,0,1:T(8,128)} %custom-call.12) | copy-start | bytes 3145732
  336.7 1.0 copy-start.4
  342.2 38.4 %copy-start.7 = (s32[2,1024]{1,0:T(2,128)S(1)}, s32[2,1024]{1,0:T(2,128)}, u32[]{:S(2)}) copy-start(s32[2,1024]{1,0:T(2,128)} %param.15) | copy-start | bytes 24580
  344.5 62.4 %all-to-all-start.1 = ((f32[4,128,1024]{2,0,1:T(4,128)}), f32[4,128,1024]{2,0,1:T(4,128)S(1)}, u32[]{:S(2)}, u32[]{:S(2)}) async-start(f32[4,128,1024]{2,0,1:T(4,128)} %pad_maximum_fusion.7), calls=%async_computation.1 | async-start | bytes 4194304 | tf_op jit(solution)/shard_map/all_to_all | solution.py:17
  408.7 5.9 %copy-start.1 = (f32[2,4,32,1024]{3,2,1,0:T(8,128)S(1)}, f32[2,4,32,1024]{3,2,1,0:T(8,128)}, u32[]{:S(2)}) copy-start(f32[2,4,32,1024]{3,2,1,0:T(8,128)} %param.12) | copy-start | bytes 3145732
  415.7 4.6 %copy-start.2 = (f32[2,4,32,1024]{3,2,1,0:T(8,128)S(1)}, f32[2,4,32,1024]{3,2,1,0:T(8,128)}, u32[]{:S(2)}) copy-start(f32[2,4,32,1024]{3,2,1,0:T(8,128)} %param.11) | copy-start | bytes 3145732
